TPU v7x, 32 devices: a whole 2x2x4 slice. The times are simulated.
32 devices in a mesh: pipe: 8 (over z, y), dp: 4 (over x, core).
Axes of the slice: x: 2, y: 2, z: 4, core: 2. Of those that a mesh axis runs over, the one named last changes fastest.
Arguments:
- grad_output: bfloat16 [512, 8192], P('dp'), may hold values from -6 to 6
- hidden: bfloat16 [512, 14336], P('dp', 'pipe'), may hold values from -6 to 6
- next_hidden: bfloat16 [512, 14336], P('dp', 'pipe'), may hold values from -6 to 6
- master: float32 [14336, 8192], P('pipe', 'dp'), may hold values from -0.046875 to 0.046875
- moment: float32 [14336, 8192], P('pipe', 'dp'), may hold values from -24 to 24
- second_moment: float32 [14336, 8192], P('pipe', 'dp'), may hold values from 5 to 100
Outputs:
- update: float32 [14336, 8192], P('pipe', 'dp')
- upstream_grad: bfloat16 [512, 14336], P('dp', 'pipe')
- next_output: bfloat16 [512, 8192], P('pipe', 'dp')
All inputs are finite; a program needn't handle non-finite values.
Results may differ from a plain program's by a relative error of at most 0.005.
Values may be sent and summed in bfloat16 or wider, within the bound.
A program may use at most 256 MiB of HBM per device.

v0:
```python
import jax
import jax.numpy as jnp
from jax import lax
from jax.sharding import PartitionSpec as P

beta_one = 0.9
beta_two = 0.95
corr_one = 1.0 - 0.9**10
corr_two = 1.0 - 0.95**10
learn_rate = 0.005
decay_rate = 0.1
epsilon = 1e-08


def on_device(grad_output, hidden, next_hidden, master, moment, second_moment):
    weights_low = master.astype(jnp.bfloat16)
    columns = lax.all_to_all(grad_output, "dp", split_axis=1, concat_axis=0, tiled=True)
    rows_part = columns
    hidden_sum = lax.psum_scatter(
        lax.dot_general(
            rows_part, weights_low, (((1,), (1,)), ((), ())), preferred_element_type=jnp.float32
        ),
        "dp",
        scatter_dimension=0,
        tiled=True,
    )
    upstream = hidden_sum.astype(jnp.bfloat16)
    gathered = lax.all_gather(hidden, "dp", axis=0, tiled=True)
    gradient = lax.dot_general(
        gathered, columns, (((0,), (0,)), ((), ())), preferred_element_type=jnp.float32
    )
    moment_new = beta_one * moment + (1.0 - beta_one) * gradient
    second_new = beta_two * second_moment + (1.0 - beta_two) * gradient * gradient
    update = -(
        moment_new / corr_one / (jnp.sqrt(second_new / corr_two) + epsilon) + decay_rate * master
    )
    fresh_low = (master + learn_rate * update).astype(jnp.bfloat16)
    later_rows = lax.all_gather(next_hidden, "dp", axis=0, tiled=True)
    rows_part = later_rows
    next_out = lax.psum_scatter(
        jnp.dot(rows_part, fresh_low, preferred_element_type=jnp.float32),
        "pipe",
        scatter_dimension=0,
        tiled=True,
    ).astype(jnp.bfloat16)
    return (update, upstream, next_out)


def solution(mesh):
    in_specs = (
        P("dp", None),
        P("dp", "pipe"),
        P("dp", "pipe"),
        P("pipe", "dp"),
        P("pipe", "dp"),
        P("pipe", "dp"),
    )
    out_specs = (P("pipe", "dp"), P("dp", "pipe"), P("pipe", "dp"))
    return jax.shard_map(
        on_device, mesh=mesh, in_specs=in_specs, out_specs=out_specs, check_vma=False
    )
```

profile of v0, /device:TPU:0, one launch (start us, length us, event | category | flops | bytes accessed | tf_op | source)
XLA Modules:
  0.0 211.2 jit_solution(2200444903130895348)
XLA Ops:
  7.2 0.0 all-gather.3.cloned.1.call-start
  7.2 0.7 all-gather.3.cloned.1.call-update
  7.9 4.1 %copy.14 = bf16[128,8192]{0,1:T(8,128)(2,1)} copy(bf16[128,8192]{1,0:T(8,128)(2,1)} %param.6) | data formatting | bytes 4194304 | tf_op args[0]
  12.0 4.2 %all-to-all-start = ((bf16[128,4,2048]{0,2,1:T(8,128)(2,1)}), bf16[128,4,2048]{0,2,1:T(8,128)(2,1)S(1)}, u32[]{:S(2)}, u32[]{:S(2)}) async-start(bf16[128,4,2048]{0,2,1:T(8,128)(2,1)} %bitcast.11), calls=%async_computation | async-start | bytes 4194304 | tf_op jit(solution)/shard_map/all_to_all | solution.py:17
  16.2 0.0 all-gather.5.cloned.1.call-start
  16.2 0.7 all-gather.5.cloned.1.call-update
  16.9 0.0 reduce-scatter.5.cloned.1.call-start
  17.0 34.7 %all-to-all-done = bf16[128,4,2048]{0,2,1:T(8,128)(2,1)S(1)} async-done(((bf16[128,4,2048]{0,2,1:T(8,128)(2,1)}), bf16[128,4,2048]{0,2,1:T(8,128)(2,1)S(1)}, u32[]{:S(2)}, u32[]{:S(2)}) %all-to-all-start) | async-done | bytes 2097184 | tf_op jit(solution)/shard_map/all_to_all | solution.py:17
  51.7 2.6 %copy.15 = bf16[4,128,2048]{2,1,0:T(8,128)(2,1)} copy(bf16[4,128,2048]{1,2,0:T(8,128)(2,1)S(1)} %bitcast.10) | data formatting | bytes 4194304 | tf_op jit(solution)/shard_map/all_to_all | solution.py:17
  54.3 0.0 copy-start
  54.3 11.8 %fusion.9 = f32[512,1792]{1,0:T(8,128)} fusion(bf16[512,2048]{1,0:T(8,128)(2,1)} %bitcast.12, f32[1792,2048]{1,0:T(8,128)} %param.9), kind=kOutput, calls=%fused_computation.11 | convolution fusion | flops 3761766400 | bytes 20447232 | tf_op jit(solution)/shard_map/dot_general | solution.py:20
  66.1 0.0 reduce-scatter.5.cloned.1.call-update
  66.1 0.2 reduce-scatter.7.cloned.1.call-start
  66.4 0.0 all-gather.3.cloned.1.call-done
  66.4 0.0 copy-done
  66.4 25.2 %fusion.6 = f32[1792,2048]{1,0:T(8,128)} fusion(f32[1792,2048]{1,0:T(8,128)} %param.9, f32[1792,2048]{1,0:T(8,128)} %param.11, f32[1792,2048]{1,0:T(8,128)} %param.10, bf16[512,1792]{1,0:T(8,128)(2,1)} %all-gather.3.cloned.1.call-done, bf16[512,2048]{1,0:T(8,128)(2,1)S(1)} %bitcast.13), kind=kOutput, calls=%fused_computation.8 | convolution fusion | flops 3809476608 | bytes 62652416 | tf_op jit(solution)/shard_map/dot_general | solution.py:29
  91.6 16.1 %fusion.11 = f32[512,2048]{0,1:T(8,128)} fusion(bf16[512,1792]{1,0:T(8,128)(2,1)} %all-gather.5.cloned.1.call-done, f32[1792,2048]{1,0:T(8,128)} %param.9, f32[1792,2048]{1,0:T(8,128)} %fusion.6), kind=kOutput, calls=%fused_computation.13 | convolution fusion | flops 3769106432 | bytes 35389440 | tf_op jit(solution)/shard_map/dot_general | solution.py:41
  107.8 5.5 %copy.17 = f32[512,2048]{1,0:T(8,128)} copy(f32[512,2048]{0,1:T(8,128)} %fusion.11) | data formatting | bytes 8388608
  113.2 0.0 reduce-scatter.7.cloned.1.call-update
  113.2 0.0 reduce-scatter.5.cloned.1.call-done
  113.3 2.0 convert_element_type.13
  115.3 87.2 %reduce-scatter.7.cloned.1.call-done = f32[64,2048]{1,0:T(8,128)} async-done(((f32[512,2048]{1,0:T(8,128)}), f32[64,2048]{1,0:T(8,128)}) %reduce-scatter.7.cloned.1.call-update) | async-done | bytes 524304
  202.5 1.3 copy.18
  203.8 0.9 copy.16
  (1 shorter events, 0.0 us)
Async XLA Ops:
  7.2 59.2 %all-gather.3.cloned.1.call-start = ((), (), s32[]{:S(2)}) async-start(), calls=%async_computation.3 | async-start | bytes 2293760 | tf_op jit(solution)/shard_map/all_gather | solution.py:28
  12.0 39.7 %all-to-all-start = ((bf16[128,4,2048]{0,2,1:T(8,128)(2,1)}), bf16[128,4,2048]{0,2,1:T(8,128)(2,1)S(1)}, u32[]{:S(2)}, u32[]{:S(2)}) async-start(bf16[128,4,2048]{0,2,1:T(8,128)(2,1)} %bitcast.11), calls=%async_computation | async-start | bytes 4194304 | tf_op jit(solution)/shard_map/all_to_all | solution.py:17
  16.2 75.4 %all-gather.5.cloned.1.call-start = ((), (), s32[]{:S(2)}) async-start(), calls=%async_computation.5 | async-start | bytes 2293760 | tf_op jit(solution)/shard_map/all_gather | solution.py:38
  16.9 96.4 %reduce-scatter.5.cloned.1.call-start = ((), (), s32[]{:S(2)}) async-start(), calls=%async_computation.4 | async-start | bytes 4587520 | tf_op jit(solution)/shard_map/reduce_scatter | solution.py:19
  54.3 12.1 %copy-start = (bf16[4,128,2048]{2,1,0:T(8,128)(2,1)S(1)}, bf16[4,128,2048]{2,1,0:T(8,128)(2,1)}, u32[]{:S(2)}) copy-start(bf16[4,128,2048]{2,1,0:T(8,128)(2,1)} %copy.15) | copy-start | bytes 6291460
  66.1 136.3 %reduce-scatter.7.cloned.1.call-start = ((), (), s32[]{:S(2)}) async-start(), calls=%async_computation.6 | async-start | bytes 4718592
Sparse Core Ops, SparseCore 0:
  9.6 33.7 all-gather.2
  44.9 21.0 all-gather.4
  68.6 41.2 reduce-scatter.4
  113.8 88.6 reduce-scatter.6
where the time goes:
time: 212 us; the launch traced here: 211 us
  waiting for transfers between devices  123 us (58%)
  matrix products  53.2 us (25%)
  local copies, waits for them, and re-layouts  14.3 us (7%)
  between operations  13.8 us (7%)
  starting transfers between devices  4.51 us (2%)
    unnamed x5, waiting for transfers between devices  88.7 us
    all_to_all x1, waiting for transfers between devices, on_device(): lax.all_to_all(grad_output, 'dp', split_axis=1, concat_axis=0, tiled=True)  34.7 us
    dot_general x1, matrix products, on_device(): lax.dot_general(gathered, columns, (((0,), (0,)), ((), ())), preferred_el...  25.2 us
    dot_general x1, matrix products, on_device(): jnp.dot(rows_part, fresh_low, preferred_element_type=jnp.float32)  16.1 us
    dot_general x1, matrix products, on_device(): lax.dot_general(rows_part, weights_low, (((1,), (1,)), ((), ())), preferr...  11.8 us
    unnamed x6, local copies, waits for them, and re-layouts  11.8 us
  transfers between devices with their start and end apart: 5, of which 2 were waited for; matrix products, arithmetic and copies ran while one was open for 32% of the time, Pallas kernels for 0%

commit v1 on v0

v1 whole, which is shorter than its diff:
```python
import functools
import math

import jax
import jax.numpy as jnp
from jax import lax
from jax.experimental import pallas as pl
from jax.experimental.pallas import tpu as pltpu
from jax.sharding import PartitionSpec as P

beta_one = 0.9
beta_two = 0.95
corr_one = 1.0 - 0.9**10
corr_two = 1.0 - 0.95**10
learn_rate = 0.005
decay_rate = 0.1
epsilon = 1e-08

f32 = jnp.float32
bf16 = jnp.bfloat16
MESH = pl.DeviceIdType.MESH
ALL = slice(None)


def remote(src, dst, send, recv, pipe, dp):
    return pltpu.make_async_remote_copy(
        src_ref=src, dst_ref=dst, send_sem=send, recv_sem=recv,
        device_id=(pipe, dp), device_id_type=MESH,
    )


def greet(partners):
    barrier = pltpu.get_barrier_semaphore()
    for partner in partners:
        pl.semaphore_signal(barrier, inc=1, device_id=partner, device_id_type=MESH)
    pl.semaphore_wait(barrier, len(partners))


def gather_kernel(n_dp, share, g, hid, nxt, cols, h, nh, loc, sib_s, sib_r,
                  g_s, g_r, gf_s, gf_r, h_s, h_r, hf_s, hf_r):
    pipe, dp = lax.axis_index("pipe"), lax.axis_index("dp")
    chips = n_dp // 2
    chip, core = dp // 2, dp % 2
    sib = chip * 2 + 1 - core
    rows, width = cols.shape[1], cols.shape[2]
    part = rows // share
    q = pipe % share
    base = pipe - q
    mine = pl.ds(pl.multiple_of(q * part, part), part)

    def columns(d):
        return pl.ds(pl.multiple_of(d * width, width), width)

    mates = [base + (q + f) % share for f in range(1, share)]
    ahead = [(chip + o) % chips for o in range(chips)]
    behind = [(chip + chips - o) % chips for o in range(chips)]
    partners = [(pipe, sib)]
    partners += [(pipe, ahead[o] * 2 + (core + e) % 2) for o in range(1, chips) for e in range(2)]
    partners += [(m, dp) for m in mates]

    local = [
        pltpu.make_async_copy(g.at[:, columns(dp)], cols.at[dp], loc.at[0]),
        pltpu.make_async_copy(hid, h.at[dp], loc.at[1]),
        pltpu.make_async_copy(nxt, nh.at[dp], loc.at[2]),
    ]
    for c in local:
        c.start()
    greet(partners)

    pairs = ((hid, h), (nxt, nh))
    cross = {}
    for o in range(1, chips):
        for e in range(2):
            d = ahead[o] * 2 + (core + e) % 2
            cross[o, e] = remote(g.at[mine, columns(d)], cols.at[dp, mine],
                                 g_s.at[o, e], g_r.at[o, e], pipe, d)
            cross[o, e].start()
    hops = {}
    for i, (src, dst) in enumerate(pairs):
        for o in range(1, chips):
            hops[i, o] = remote(src, dst.at[dp], h_s.at[i, o], h_r.at[i, o],
                                pipe, ahead[o] * 2 + core)
            hops[i, o].start()
    side = [remote(g.at[:, columns(sib)], cols.at[dp], sib_s.at[0], sib_r.at[0], pipe, sib)]
    for i, (src, dst) in enumerate(pairs):
        side.append(remote(src, dst.at[dp], sib_s.at[i + 1], sib_r.at[i + 1], pipe, sib))
    for c in side:
        c.start()
    passed = []
    for o in range(1, chips):
        for e in range(2):
            cross[o, e].wait_recv()
            block = cols.at[behind[o] * 2 + (core + e) % 2, mine]
            for f, m in enumerate(mates):
                c = remote(block, block, gf_s.at[o, e, f], gf_r.at[o, e, f], m, dp)
                c.start()
                passed.append(c)
    for i, (src, dst) in enumerate(pairs):
        for o in range(1, chips):
            hops[i, o].wait_recv()
            block = dst.at[behind[o] * 2 + core]
            c = remote(block, block, hf_s.at[i, o], hf_r.at[i, o], pipe, sib)
            c.start()
            passed.append(c)
    for c in local:
        c.wait()
    for c in list(cross.values()) + list(hops.values()):
        c.wait_send()
    for c in side + passed:
        c.wait()


def gather(n_pipe, n_dp, g, hid, nxt):
    rows, ff = hid.shape
    width = g.shape[1] // n_dp
    chips = n_dp // 2
    share = 4 if n_pipe % 4 == 0 else 1
    anywhere = pl.BlockSpec(memory_space=pl.ANY)
    dma = pltpu.SemaphoreType.DMA
    mates = max(share - 1, 1)
    outs = pl.pallas_call(
        functools.partial(gather_kernel, n_dp, share),
        out_shape=[jax.ShapeDtypeStruct((n_dp, rows, w), bf16) for w in (width, ff, ff)],
        in_specs=[anywhere] * 3,
        out_specs=[anywhere] * 3,
        scratch_shapes=[
            dma((3,)), dma((3,)), dma((3,)),
            dma((chips, 2)), dma((chips, 2)),
            dma((chips, 2, mates)), dma((chips, 2, mates)),
            dma((2, chips)), dma((2, chips)), dma((2, chips)), dma((2, chips)),
        ],
        compiler_params=pltpu.CompilerParams(collective_id=1, has_side_effects=True),
        name="gather_all",
    )(g, hid, nxt)
    return [o.reshape(n_dp * rows, o.shape[2]) for o in outs]


def step_kernel(chunk, g_ref, h_ref, nh_ref, w_ref, m_ref, s_ref,
                up_ref, next_ref, update_ref, turned, total, fresh):
    j = pl.program_id(0)
    ff = h_ref.shape[1]

    @pl.when(j == 0)
    def _():
        total[...] = jnp.zeros_like(total)
        for c in range(0, ff, chunk):
            turned[pl.ds(c, chunk), :] = h_ref[:, pl.ds(c, chunk)].T

    for c in range(0, ff, chunk):
        r = pl.ds(c, chunk)
        grad = jnp.dot(turned[r, :], g_ref[...], preferred_element_type=f32)
        w = w_ref[r, :]
        total[:, r] += lax.dot_general(
            g_ref[...], w.astype(bf16), (((1,), (1,)), ((), ())), preferred_element_type=f32
        )
        top = (beta_one / corr_one) * m_ref[r, :] + ((1.0 - beta_one) / corr_one) * grad
        var = (beta_two / corr_two) * s_ref[r, :] + ((1.0 - beta_two) / corr_two) * (grad * grad)
        update = -(top / (var * lax.rsqrt(var) + epsilon) + decay_rate * w)
        update_ref[r, :] = update
        fresh[r, :] = (w + learn_rate * update).astype(bf16)
    next_ref[...] = jnp.dot(nh_ref[...], fresh[...], preferred_element_type=f32).astype(bf16)

    @pl.when(j == pl.num_programs(0) - 1)
    def _():
        up_ref[...] = total[...].astype(bf16)


def step(cols, h, nh, master, moment, second):
    tokens, width = cols.shape
    ff = h.shape[1]
    bn = 256 if width % 256 == 0 else width
    chunk = 256 if ff % 256 == 0 else 128
    whole = pl.BlockSpec((tokens, ff), lambda j: (0, 0), pipeline_mode=pl.Buffered(1))
    tall = pl.BlockSpec((ff, bn), lambda j: (0, j))
    slab = pl.BlockSpec((tokens, bn), lambda j: (0, j))
    return pl.pallas_call(
        functools.partial(step_kernel, chunk),
        grid=(width // bn,),
        out_shape=[
            jax.ShapeDtypeStruct((tokens, ff), bf16),
            jax.ShapeDtypeStruct((tokens, width), bf16),
            jax.ShapeDtypeStruct((ff, width), f32),
        ],
        in_specs=[slab, whole, whole, tall, tall, tall],
        out_specs=[pl.BlockSpec((tokens, ff), lambda j: (0, 0)), slab, tall],
        scratch_shapes=[
            pltpu.VMEM((ff, tokens), bf16),
            pltpu.VMEM((tokens, ff), f32),
            pltpu.VMEM((ff, bn), bf16),
        ],
        cost_estimate=pl.CostEstimate(
            flops=6 * tokens * ff * width, bytes_accessed=16 * ff * width, transcendentals=ff * width
        ),
        compiler_params=pltpu.CompilerParams(vmem_limit_bytes=56 << 20),
        name="fused_step",
    )(cols, h, nh, master, moment, second)


def reduce_kernel(levels, n_dp, pieces, up, nxt, up_out, next_out, *scratch):
    up_in, up_mid, up_far, us_s, us_r, uf_s, uf_r, n_s, n_r = scratch[:9]
    recv = scratch[9:9 + levels]
    send = (None,) + scratch[9 + levels:8 + 2 * levels]
    keep = (None,) + scratch[8 + 2 * levels:]
    pipe, dp = lax.axis_index("pipe"), lax.axis_index("dp")
    chips = n_dp // 2
    chip, core = dp // 2, dp % 2
    sib = chip * 2 + 1 - core
    ahead = [(chip + o) % chips for o in range(chips)]
    bit = [(pipe // 2**b) % 2 for b in range(levels)]
    across = [pipe + (1 - 2 * bit[b]) * 2**b for b in range(levels)]
    greet([(pipe, sib)] + [(pipe, ahead[o] * 2 + core) for o in range(1, chips)]
          + [(across[b], dp) for b in range(levels)])

    cw = next_out.shape[1] // pieces
    orders = []
    for k in range(pieces):
        order = list(range(levels))
        if k % 2 and levels > 1:
            order[0], order[1] = order[1], order[0]
        orders.append(order)

    def pick(k, j, value):
        left = sorted(orders[k][j:], reverse=True)
        at = left.index(orders[k][j])
        return (ALL,) * at + (value,) + (ALL,) * (len(left) - 1 - at)

    def spot(j, k):
        return (ALL,) * (levels - 1 - j) + (ALL, pl.ds(k * cw, cw))

    flights = {}

    def launch(j, k, src):
        b = orders[k][j]
        flights[j, k] = remote(src, recv[j].at[spot(j, k)], n_s.at[j, k], n_r.at[j, k], across[b], dp)
        flights[j, k].start()

    tail = lambda k: (ALL, pl.ds(k * cw, cw))
    for k in range(pieces):
        launch(0, k, nxt.at[pick(k, 0, 1 - bit[orders[k][0]]) + tail(k)])
    near = {}
    for o in list(range(1, chips)) + [0]:
        near[o] = remote(up.at[ahead[o], 1 - core], up_in.at[o], us_s.at[o], us_r.at[o], pipe, sib)
        near[o].start()
    far = {}
    for o in range(1, chips):
        near[o].wait_recv()
        up_mid[o] = (up[ahead[o], core].astype(f32) + up_in[o].astype(f32)).astype(bf16)
        far[o] = remote(up_mid.at[o], up_far.at[o], uf_s.at[o], uf_r.at[o], pipe, ahead[o] * 2 + core)
        far[o].start()

    for j in range(levels):
        for k in range(pieces):
            flights[j, k].wait_recv()

            def summed(index):
                if j == 0:
                    mine = pick(k, 0, bit[orders[k][0]])
                    full, i = [], iter(index)
                    for m in mine:
                        full.append(next(i) if isinstance(m, slice) else m)
                    kept = nxt[tuple(full) + tail(k)]
                else:
                    kept = keep[j][index + tail(k)]
                return kept.astype(f32) + recv[j][index + tail(k)].astype(f32)

            if j < levels - 1:
                b = bit[orders[k][j + 1]]
                send[j + 1][spot(j + 1, k)] = summed(pick(k, j + 1, 1 - b)).astype(bf16)
                launch(j + 1, k, send[j + 1].at[spot(j + 1, k)])
                keep[j + 1][spot(j + 1, k)] = summed(pick(k, j + 1, b))
            else:
                next_out[tail(k)] = summed(()).astype(bf16)

    near[0].wait_recv()
    total = up[chip, core].astype(f32) + up_in[0].astype(f32)
    for o in range(1, chips):
        far[o].wait_recv()
        total = total + up_far[o].astype(f32)
    up_out[...] = total.astype(bf16)
    for c in list(near.values()) + list(far.values()) + list(flights.values()):
        c.wait_send()


def reduce(n_pipe, n_dp, up, nxt):
    levels = int(math.log2(n_pipe))
    tokens, ff = up.shape
    width = nxt.shape[1]
    rows, few = tokens // n_dp, tokens // n_pipe
    chips = n_dp // 2
    pieces = 4 if width % 512 == 0 else 1
    dma = pltpu.SemaphoreType.DMA
    vmem = pl.BlockSpec(memory_space=pltpu.VMEM)
    shape = lambda j: (2,) * (levels - 1 - j) + (few, width)
    return pl.pallas_call(
        functools.partial(reduce_kernel, levels, n_dp, pieces),
        out_shape=[
            jax.ShapeDtypeStruct((rows, ff), bf16),
            jax.ShapeDtypeStruct((few, width), bf16),
        ],
        in_specs=[vmem] * 2,
        out_specs=[vmem] * 2,
        scratch_shapes=[pltpu.VMEM((chips, rows, ff), bf16)] * 3
        + [dma((chips,))] * 4
        + [dma((levels, pieces))] * 2
        + [pltpu.VMEM(shape(j), bf16) for j in range(levels)]
        + [pltpu.VMEM(shape(j), bf16) for j in range(1, levels)]
        + [pltpu.VMEM(shape(j), f32) for j in range(1, levels)],
        compiler_params=pltpu.CompilerParams(
            collective_id=2, has_side_effects=True, vmem_limit_bytes=48 << 20
        ),
        name="reduce_both",
    )(up.reshape(chips, 2, rows, ff), nxt.reshape((2,) * levels + (few, width)))


def on_device(n_pipe, n_dp, grad_output, hidden, next_hidden, master, moment, second_moment):
    cols, h, nh = gather(n_pipe, n_dp, grad_output, hidden, next_hidden)
    up, nxt, update = step(cols, h, nh, master, moment, second_moment)
    upstream, next_out = reduce(n_pipe, n_dp, up, nxt)
    return (update, upstream, next_out)


def solution(mesh):
    in_specs = (
        P("dp", None),
        P("dp", "pipe"),
        P("dp", "pipe"),
        P("pipe", "dp"),
        P("pipe", "dp"),
        P("pipe", "dp"),
    )
    out_specs = (P("pipe", "dp"), P("dp", "pipe"), P("pipe", "dp"))
    return jax.shard_map(
        functools.partial(on_device, mesh.shape["pipe"], mesh.shape["dp"]),
        mesh=mesh, in_specs=in_specs, out_specs=out_specs, check_vma=False,
    )
```

time: 212 us -> 115 us (0.54)
  waiting for transfers between devices: 123 us -> 0 us
  Pallas kernels: 0 us -> 109 us
  matrix products: 53.2 us -> 0 us
  between operations: 13.8 us -> 0.65 us
  local copies, waits for them, and re-layouts: 14.3 us -> 4.56 us
  starting transfers between devices: 4.51 us -> 0 us
    pallas_call x0 -> x3, Pallas kernels: none -> 109 us  [the longest x1 45.4 us: gather(): pl.pallas_call(functools.partial(gather_kernel, n_dp, share), out_shape=[...]
    unnamed x5 -> x0, waiting for transfers between devices: 88.7 us -> none
    dot_general x3 -> x0, matrix products: 53.2 us -> none  [the longest x1 25.2 us: on_device(): lax.dot_general(gathered, columns, (((0,), (0,)), ((), ())), preferred_el...]
    all_to_all x1 -> x0, waiting for transfers between devices: 34.7 us -> none  [on_device(): lax.all_to_all(grad_output, 'dp', split_axis=1, concat_axis=0, tiled=True)]
    unnamed x6, local copies, waits for them, and re-layouts: 11.8 us -> 4.56 us
    all_to_all x1 -> x0, starting transfers between devices: 4.21 us -> none  [on_device(): lax.all_to_all(grad_output, 'dp', split_axis=1, concat_axis=0, tiled=True)]
    all_to_all x1 -> x0, local copies, waits for them, and re-layouts: 2.58 us -> none  [on_device(): lax.all_to_all(grad_output, 'dp', split_axis=1, concat_axis=0, tiled=True)]
  transfers between devices with their start and end apart: 5 -> 0, of which waited for: 2 -> 0; matrix products, arithmetic and copies ran while one was open for 32% -> 0% of each run, Pallas kernels for 0% -> 0%
where the time goes in v1:
time: 115 us; the launch traced here: 114 us
  Pallas kernels  109 us (95%)
  local copies, waits for them, and re-layouts  4.56 us (4%)
    pallas_call x1, Pallas kernels, gather(): pl.pallas_call(functools.partial(gather_kernel, n_dp, share), out_shape=[...  45.4 us
    pallas_call x1, Pallas kernels, reduce(): pl.pallas_call(functools.partial(reduce_kernel, levels, n_dp, pieces), ou...  33.4 us
    pallas_call x1, Pallas kernels, step(): pl.pallas_call(functools.partial(step_kernel, chunk), grid=(width // bn,)...  30.4 us
    unnamed x6, local copies, waits for them, and re-layouts  4.56 us

profile of v1, /device:TPU:0, one launch (start us, length us, event | category | flops | bytes accessed | tf_op | source)
XLA Modules:
  0.0 114.4 jit_solution(13706950489291384666)
XLA Ops:
  0.6 45.4 %gather_all.1 = (bf16[4,128,2048]{2,1,0:T(8,128)(2,1)}, bf16[4,128,1792]{2,1,0:T(8,128)(2,1)}, bf16[4,128,1792]{2,1,0:T(8,128)(2,1)}) custom-call(bf16[128,8192]{1,0:T(8,128)(2,1)} %g.1, bf16[128,1792]{1,0:T(8,128)(2,1)} %hid.1, bf16[128,1792]{1,0:T(8,128)(2,1)} %nxt.1), custom_call_target="tpu_custom_call" | custom-call | tf_op jit(solution)/shard_map/gather_all/pallas_call | solution.py:121
  46.0 30.4 %fused_step.1 = (bf16[512,1792]{1,0:T(8,128)(2,1)}, bf16[512,2048]{1,0:T(8,128)(2,1)}, f32[1792,2048]{1,0:T(8,128)}) custom-call(bf16[512,2048]{1,0:T(8,128)(2,1)} %bitcast.7, bf16[512,1792]{1,0:T(8,128)(2,1)} %bitcast.8, bf16[512,1792]{1,0:T(8,128)(2,1)} %bitcast.9, f32[1792,2048]{1,0:T(8,128)} %w_ref.1, f32[1792,2048]{1,0:T(8,128)} %m_ref.1, ...), custom_call_target="tpu_custom_call" | custom-call | flops 11274289152 | bytes 58720256 | tf_op jit(solution)/shard_map/fused_step/pallas_call | solution.py:176
  76.4 0.0 copy-start
  76.4 1.6 %copy-done = bf16[512,2048]{1,0:T(8,128)(2,1)S(1)} copy-done((bf16[512,2048]{1,0:T(8,128)(2,1)S(1)}, bf16[512,2048]{1,0:T(8,128)(2,1)}, u32[]{:S(2)}) %copy-start) | copy-done | bytes 2097176
  78.0 0.0 copy-start.1
  78.0 1.5 %copy-done.1 = bf16[512,1792]{1,0:T(8,128)(2,1)S(1)} copy-done((bf16[512,1792]{1,0:T(8,128)(2,1)S(1)}, bf16[512,1792]{1,0:T(8,128)(2,1)}, u32[]{:S(2)}) %copy-start.1) | copy-done | bytes 1835032
  79.5 33.4 %reduce_both.1 = (bf16[128,1792]{1,0:T(8,128)(2,1)S(1)}, bf16[64,2048]{1,0:T(8,128)(2,1)S(1)}) custom-call(bf16[2,2,128,1792]{3,2,1,0:T(8,128)(2,1)S(1)} %bitcast.6, bf16[2,2,2,64,2048]{4,3,2,1,0:T(8,128)(2,1)S(1)} %bitcast.5), custom_call_target="tpu_custom_call" | custom-call | tf_op jit(solution)/shard_map/reduce_both/pallas_call | solution.py:294
  113.0 0.8 copy.11
  113.7 0.7 copy.12
Async XLA Ops:
  76.4 1.6 %copy-start = (bf16[512,2048]{1,0:T(8,128)(2,1)S(1)}, bf16[512,2048]{1,0:T(8,128)(2,1)}, u32[]{:S(2)}) copy-start(bf16[512,2048]{1,0:T(8,128)(2,1)} %get-tuple-element.16) | copy-start | bytes 6291460
  78.0 1.5 %copy-start.1 = (bf16[512,1792]{1,0:T(8,128)(2,1)S(1)}, bf16[512,1792]{1,0:T(8,128)(2,1)}, u32[]{:S(2)}) copy-start(bf16[512,1792]{1,0:T(8,128)(2,1)} %get-tuple-element.15) | copy-start | bytes 5505028

commit v2 on v1

--- a/solution.py
+++ b/solution.py
@@ -36,7 +36,7 @@
     pl.semaphore_wait(barrier, len(partners))
 
 
-def gather_kernel(n_dp, share, g, hid, nxt, cols, h, nh, loc, sib_s, sib_r,
+def gather_kernel(n_dp, share, g, hid, cols, h, loc, sib_s, sib_r,
                   g_s, g_r, gf_s, gf_r, h_s, h_r, hf_s, hf_r):
     pipe, dp = lax.axis_index("pipe"), lax.axis_index("dp")
     chips = n_dp // 2
@@ -61,13 +61,11 @@
     local = [
         pltpu.make_async_copy(g.at[:, columns(dp)], cols.at[dp], loc.at[0]),
         pltpu.make_async_copy(hid, h.at[dp], loc.at[1]),
-        pltpu.make_async_copy(nxt, nh.at[dp], loc.at[2]),
     ]
     for c in local:
         c.start()
     greet(partners)
 
-    pairs = ((hid, h), (nxt, nh))
     cross = {}
     for o in range(1, chips):
         for e in range(2):
@@ -75,15 +73,18 @@
             cross[o, e] = remote(g.at[mine, columns(d)], cols.at[dp, mine],
                                  g_s.at[o, e], g_r.at[o, e], pipe, d)
             cross[o, e].start()
+    half = rows // 2
     hops = {}
-    for i, (src, dst) in enumerate(pairs):
-        for o in range(1, chips):
-            hops[i, o] = remote(src, dst.at[dp], h_s.at[i, o], h_r.at[i, o],
+    for o in range(1, chips):
+        for i in range(2):
+            some = pl.ds(i * half, half)
+            hops[o, i] = remote(hid.at[some], h.at[dp, some], h_s.at[o, i], h_r.at[o, i],
                                 pipe, ahead[o] * 2 + core)
-            hops[i, o].start()
-    side = [remote(g.at[:, columns(sib)], cols.at[dp], sib_s.at[0], sib_r.at[0], pipe, sib)]
-    for i, (src, dst) in enumerate(pairs):
-        side.append(remote(src, dst.at[dp], sib_s.at[i + 1], sib_r.at[i + 1], pipe, sib))
+            hops[o, i].start()
+    side = [
+        remote(g.at[:, columns(sib)], cols.at[dp], sib_s.at[0], sib_r.at[0], pipe, sib),
+        remote(hid, h.at[dp], sib_s.at[1], sib_r.at[1], pipe, sib),
+    ]
     for c in side:
         c.start()
     passed = []
@@ -95,11 +96,11 @@
                 c = remote(block, block, gf_s.at[o, e, f], gf_r.at[o, e, f], m, dp)
                 c.start()
                 passed.append(c)
-    for i, (src, dst) in enumerate(pairs):
-        for o in range(1, chips):
-            hops[i, o].wait_recv()
-            block = dst.at[behind[o] * 2 + core]
-            c = remote(block, block, hf_s.at[i, o], hf_r.at[i, o], pipe, sib)
+    for o in range(1, chips):
+        for i in range(2):
+            hops[o, i].wait_recv()
+            block = h.at[behind[o] * 2 + core, pl.ds(i * half, half)]
+            c = remote(block, block, hf_s.at[o, i], hf_r.at[o, i], pipe, sib)
             c.start()
             passed.append(c)
     for c in local:
@@ -110,33 +111,32 @@
         c.wait()
 
 
-def gather(n_pipe, n_dp, g, hid, nxt):
+def gather(n_pipe, n_dp, g, hid, share):
     rows, ff = hid.shape
     width = g.shape[1] // n_dp
     chips = n_dp // 2
-    share = 4 if n_pipe % 4 == 0 else 1
     anywhere = pl.BlockSpec(memory_space=pl.ANY)
     dma = pltpu.SemaphoreType.DMA
     mates = max(share - 1, 1)
     outs = pl.pallas_call(
         functools.partial(gather_kernel, n_dp, share),
-        out_shape=[jax.ShapeDtypeStruct((n_dp, rows, w), bf16) for w in (width, ff, ff)],
-        in_specs=[anywhere] * 3,
-        out_specs=[anywhere] * 3,
+        out_shape=[jax.ShapeDtypeStruct((n_dp, rows, w), bf16) for w in (width, ff)],
+        in_specs=[anywhere] * 2,
+        out_specs=[anywhere] * 2,
         scratch_shapes=[
-            dma((3,)), dma((3,)), dma((3,)),
+            dma((2,)), dma((2,)), dma((2,)),
             dma((chips, 2)), dma((chips, 2)),
             dma((chips, 2, mates)), dma((chips, 2, mates)),
-            dma((2, chips)), dma((2, chips)), dma((2, chips)), dma((2, chips)),
+            dma((chips, 2)), dma((chips, 2)), dma((chips, 2)), dma((chips, 2)),
         ],
         compiler_params=pltpu.CompilerParams(collective_id=1, has_side_effects=True),
         name="gather_all",
-    )(g, hid, nxt)
+    )(g, hid)
     return [o.reshape(n_dp * rows, o.shape[2]) for o in outs]
 
 
-def step_kernel(chunk, g_ref, h_ref, nh_ref, w_ref, m_ref, s_ref,
-                up_ref, next_ref, update_ref, turned, total, fresh):
+def step_kernel(chunk, g_ref, h_ref, w_ref, m_ref, s_ref,
+                up_ref, fresh, update_ref, turned, total):
     j = pl.program_id(0)
     ff = h_ref.shape[1]
 
@@ -158,17 +158,16 @@
         update = -(top / (var * lax.rsqrt(var) + epsilon) + decay_rate * w)
         update_ref[r, :] = update
         fresh[r, :] = (w + learn_rate * update).astype(bf16)
-    next_ref[...] = jnp.dot(nh_ref[...], fresh[...], preferred_element_type=f32).astype(bf16)
 
     @pl.when(j == pl.num_programs(0) - 1)
     def _():
         up_ref[...] = total[...].astype(bf16)
 
 
-def step(cols, h, nh, master, moment, second):
+def step(cols, h, master, moment, second):
     tokens, width = cols.shape
     ff = h.shape[1]
-    bn = 256 if width % 256 == 0 else width
+    bn = 512 if width % 512 == 0 else width
     chunk = 256 if ff % 256 == 0 else 128
     whole = pl.BlockSpec((tokens, ff), lambda j: (0, 0), pipeline_mode=pl.Buffered(1))
     tall = pl.BlockSpec((ff, bn), lambda j: (0, j))
@@ -178,25 +177,27 @@
         grid=(width // bn,),
         out_shape=[
             jax.ShapeDtypeStruct((tokens, ff), bf16),
-            jax.ShapeDtypeStruct((tokens, width), bf16),
+            jax.ShapeDtypeStruct((ff, width), bf16),
             jax.ShapeDtypeStruct((ff, width), f32),
         ],
-        in_specs=[slab, whole, whole, tall, tall, tall],
-        out_specs=[pl.BlockSpec((tokens, ff), lambda j: (0, 0)), slab, tall],
+        in_specs=[slab, whole, tall, tall, tall],
+        out_specs=[pl.BlockSpec((tokens, ff), lambda j: (0, 0)), tall, tall],
         scratch_shapes=[
             pltpu.VMEM((ff, tokens), bf16),
             pltpu.VMEM((tokens, ff), f32),
-            pltpu.VMEM((ff, bn), bf16),
         ],
         cost_estimate=pl.CostEstimate(
-            flops=6 * tokens * ff * width, bytes_accessed=16 * ff * width, transcendentals=ff * width
+            flops=4 * tokens * ff * width, bytes_accessed=18 * ff * width, transcendentals=ff * width
         ),
         compiler_params=pltpu.CompilerParams(vmem_limit_bytes=56 << 20),
         name="fused_step",
-    )(cols, h, nh, master, moment, second)
-
-
-def reduce_kernel(levels, n_dp, pieces, up, nxt, up_out, next_out, *scratch):
+    )(cols, h, master, moment, second)
+
+
+def reduce_kernel(levels, n_dp, pieces, up_hbm, fresh_hbm, *refs):
+    nh_hbm, up_out, next_out = refs[:n_dp], refs[n_dp], refs[n_dp + 1]
+    up, nh, fresh, nxt, loc = refs[n_dp + 2:n_dp + 7]
+    scratch = refs[n_dp + 7:]
     up_in, up_mid, up_far, us_s, us_r, uf_s, uf_r, n_s, n_r = scratch[:9]
     recv = scratch[9:9 + levels]
     send = (None,) + scratch[9 + levels:8 + 2 * levels]
@@ -208,10 +209,21 @@
     ahead = [(chip + o) % chips for o in range(chips)]
     bit = [(pipe // 2**b) % 2 for b in range(levels)]
     across = [pipe + (1 - 2 * bit[b]) * 2**b for b in range(levels)]
+    cw = next_out.shape[1] // pieces
+    rows = nh_hbm[0].shape[0]
+    later = []
+    for o in range(n_dp):
+        at = pl.multiple_of((dp + n_dp - o) % n_dp * rows, rows)
+        later.append(pltpu.make_async_copy(nh_hbm[o], nh.at[pl.ds(at, rows)], loc.at[1 + pieces + o]))
+    loads = [pltpu.make_async_copy(up_hbm.at[:, core], up, loc.at[0])]
+    loads += [pltpu.make_async_copy(fresh_hbm.at[:, pl.ds(k * cw, cw)],
+                                    fresh.at[:, pl.ds(k * cw, cw)], loc.at[1 + k])
+              for k in range(pieces)]
+    for c in later + loads[1:] + loads[:1]:
+        c.start()
     greet([(pipe, sib)] + [(pipe, ahead[o] * 2 + core) for o in range(1, chips)]
           + [(across[b], dp) for b in range(levels)])
 
-    cw = next_out.shape[1] // pieces
     orders = []
     for k in range(pieces):
         order = list(range(levels))
@@ -234,17 +246,27 @@
         flights[j, k] = remote(src, recv[j].at[spot(j, k)], n_s.at[j, k], n_r.at[j, k], across[b], dp)
         flights[j, k].start()
 
+    half = nh.shape[0] // 2
     tail = lambda k: (ALL, pl.ds(k * cw, cw))
-    for k in range(pieces):
-        launch(0, k, nxt.at[pick(k, 0, 1 - bit[orders[k][0]]) + tail(k)])
     near = {}
     for o in list(range(1, chips)) + [0]:
-        near[o] = remote(up.at[ahead[o], 1 - core], up_in.at[o], us_s.at[o], us_r.at[o], pipe, sib)
+        near[o] = remote(up_hbm.at[ahead[o], 1 - core], up_in.at[o], us_s.at[o], us_r.at[o], pipe, sib)
         near[o].start()
+    for c in later:
+        c.wait()
+    for k in range(pieces):
+        loads[1 + k].wait()
+        for t in range(2):
+            product = jnp.dot(nh[pl.ds(t * half, half), :], fresh[:, pl.ds(k * cw, cw)],
+                              preferred_element_type=f32).astype(bf16)
+            nxt[(t,) + (ALL,) * levels + (pl.ds(k * cw, cw),)] = product.reshape(
+                (2,) * (levels - 1) + (half // 2 ** (levels - 1), cw))
+        launch(0, k, nxt.at[pick(k, 0, 1 - bit[orders[k][0]]) + tail(k)])
+    loads[0].wait()
     far = {}
     for o in range(1, chips):
         near[o].wait_recv()
-        up_mid[o] = (up[ahead[o], core].astype(f32) + up_in[o].astype(f32)).astype(bf16)
+        up_mid[o] = (up[ahead[o]].astype(f32) + up_in[o].astype(f32)).astype(bf16)
         far[o] = remote(up_mid.at[o], up_far.at[o], uf_s.at[o], uf_r.at[o], pipe, ahead[o] * 2 + core)
         far[o].start()
 
@@ -272,7 +294,7 @@
                 next_out[tail(k)] = summed(()).astype(bf16)
 
     near[0].wait_recv()
-    total = up[chip, core].astype(f32) + up_in[0].astype(f32)
+    total = up[chip].astype(f32) + up_in[0].astype(f32)
     for o in range(1, chips):
         far[o].wait_recv()
         total = total + up_far[o].astype(f32)
@@ -281,15 +303,16 @@
         c.wait_send()
 
 
-def reduce(n_pipe, n_dp, up, nxt):
+def reduce(n_pipe, n_dp, up, nh, fresh):
     levels = int(math.log2(n_pipe))
     tokens, ff = up.shape
-    width = nxt.shape[1]
+    width = fresh.shape[1]
     rows, few = tokens // n_dp, tokens // n_pipe
     chips = n_dp // 2
-    pieces = 4 if width % 512 == 0 else 1
+    pieces = 8 if width % 2048 == 0 else 4 if width % 512 == 0 else 1
     dma = pltpu.SemaphoreType.DMA
     vmem = pl.BlockSpec(memory_space=pltpu.VMEM)
+    hbm = pl.BlockSpec(memory_space=pltpu.HBM)
     shape = lambda j: (2,) * (levels - 1 - j) + (few, width)
     return pl.pallas_call(
         functools.partial(reduce_kernel, levels, n_dp, pieces),
@@ -297,25 +320,37 @@
             jax.ShapeDtypeStruct((rows, ff), bf16),
             jax.ShapeDtypeStruct((few, width), bf16),
         ],
-        in_specs=[vmem] * 2,
+        in_specs=[hbm] * (2 + n_dp),
         out_specs=[vmem] * 2,
-        scratch_shapes=[pltpu.VMEM((chips, rows, ff), bf16)] * 3
+        scratch_shapes=[
+            pltpu.VMEM((chips, rows, ff), bf16),
+            pltpu.VMEM((tokens, ff), bf16),
+            pltpu.VMEM((ff, width), bf16),
+            pltpu.VMEM((2,) * levels + (few, width), bf16),
+            dma((1 + pieces + n_dp,)),
+        ]
+        + [pltpu.VMEM((chips, rows, ff), bf16)] * 3
         + [dma((chips,))] * 4
         + [dma((levels, pieces))] * 2
         + [pltpu.VMEM(shape(j), bf16) for j in range(levels)]
         + [pltpu.VMEM(shape(j), bf16) for j in range(1, levels)]
         + [pltpu.VMEM(shape(j), f32) for j in range(1, levels)],
         compiler_params=pltpu.CompilerParams(
-            collective_id=2, has_side_effects=True, vmem_limit_bytes=48 << 20
+            collective_id=2, has_side_effects=True, vmem_limit_bytes=62 << 20
         ),
         name="reduce_both",
-    )(up.reshape(chips, 2, rows, ff), nxt.reshape((2,) * levels + (few, width)))
+    )(up.reshape(chips, 2, rows, ff), fresh, *nh)
 
 
 def on_device(n_pipe, n_dp, grad_output, hidden, next_hidden, master, moment, second_moment):
-    cols, h, nh = gather(n_pipe, n_dp, grad_output, hidden, next_hidden)
-    up, nxt, update = step(cols, h, nh, master, moment, second_moment)
-    upstream, next_out = reduce(n_pipe, n_dp, up, nxt)
+    share = 4 if n_pipe % 4 == 0 else 1
+    cols, h = gather(n_pipe, n_dp, grad_output, hidden, share)
+    later, cols = lax.optimization_barrier((next_hidden, cols))
+    nh = [later] + [
+        lax.ppermute(later, "dp", [(i, (i + o) % n_dp) for i in range(n_dp)]) for o in range(1, n_dp)
+    ]
+    up, fresh, update = step(cols, h, master, moment, second_moment)
+    upstream, next_out = reduce(n_pipe, n_dp, up, nh, fresh)
     return (update, upstream, next_out)
 
 

time: 115 us -> 103 us (0.90)
  Pallas kernels: 109 us -> 92.8 us
  starting transfers between devices: 0 us -> 4.46 us
    pallas_call x1, Pallas kernels: 45.4 us -> 31.4 us  [gather(): pl.pallas_call(functools.partial(gather_kernel, n_dp, share), out_shape=[...]
    ppermute x0 -> x3, starting transfers between devices: none -> 4.46 us  [on_device(): lax.ppermute(later, 'dp', [(i, (i + o) % n_dp) for i in range(n_dp)])]
    pallas_call x1, Pallas kernels: 30.4 us -> 27.8 us  [step(): pl.pallas_call(functools.partial(step_kernel, chunk), grid=(width // bn,)...]
    unnamed x6 -> x8, local copies, waits for them, and re-layouts: 4.56 us -> 4.54 us
  transfers between devices with their start and end apart: 0 -> 3, of which waited for: 0 -> 0; matrix products, arithmetic and copies ran while one was open for 0% -> 0% of each run, Pallas kernels for 0% -> 27%
where the time goes in v2:
time: 103 us; the launch traced here: 102 us
  Pallas kernels  92.8 us (90%)
  local copies, waits for them, and re-layouts  4.54 us (4%)
  starting transfers between devices  4.46 us (4%)
    pallas_call x1, Pallas kernels, reduce(): pl.pallas_call(functools.partial(reduce_kernel, levels, n_dp, pieces), ou...  33.6 us
    pallas_call x1, Pallas kernels, gather(): pl.pallas_call(functools.partial(gather_kernel, n_dp, share), out_shape=[...  31.4 us
    pallas_call x1, Pallas kernels, step(): pl.pallas_call(functools.partial(step_kernel, chunk), grid=(width // bn,)...  27.8 us
    unnamed x8, local copies, waits for them, and re-layouts  4.54 us
    ppermute x3, starting transfers between devices, on_device(): lax.ppermute(later, 'dp', [(i, (i + o) % n_dp) for i in range(n_dp)])  4.46 us
  transfers between devices with their start and end apart: 3, of which 0 were waited for; matrix products, arithmetic and copies ran while one was open for 0% of the time, Pallas kernels for 27%

profile of v2, /device:TPU:0, one launch (start us, length us, event | category | flops | bytes accessed | tf_op | source)
XLA Modules:
  0.0 102.5 jit_solution(15031549001235500)
XLA Ops:
  0.6 31.4 %gather_all.1 = (bf16[4,128,2048]{2,1,0:T(8,128)(2,1)}, bf16[4,128,1792]{2,1,0:T(8,128)(2,1)}) custom-call(bf16[128,8192]{1,0:T(8,128)(2,1)} %g.1, bf16[128,1792]{1,0:T(8,128)(2,1)} %hid.1), custom_call_target="tpu_custom_call" | custom-call | tf_op jit(solution)/shard_map/gather_all/pallas_call | solution.py:121
  32.1 0.5 collective-permute-start
  32.6 2.6 %collective-permute-start.1 = (bf16[128,1792]{1,0:T(8,128)(2,1)}, bf16[128,1792]{1,0:T(8,128)(2,1)S(1)}, u32[]{:S(2)}, u32[]{:S(2)}) collective-permute-start(bf16[128,1792]{1,0:T(8,128)(2,1)} %refs_0_), channel_id=1, source_target_pairs={{0,2},{1,3},{2,0},{3,1},{4,6},{5,7},{6,4},{7,5},{8,10},{9,11},{10,... | collective-permute-start | bytes 1376264 | tf_op jit(solution)/shard_map/ppermute | solution.py:350
  35.1 1.4 %collective-permute-start.2 = (bf16[128,1792]{1,0:T(8,128)(2,1)}, bf16[128,1792]{1,0:T(8,128)(2,1)S(1)}, u32[]{:S(2)}, u32[]{:S(2)}) collective-permute-start(bf16[128,1792]{1,0:T(8,128)(2,1)} %refs_0_), channel_id=1, source_target_pairs={{0,3},{1,0},{2,1},{3,2},{4,7},{5,4},{6,5},{7,6},{8,11},{9,8},{10,9... | collective-permute-start | bytes 1376264 | tf_op jit(solution)/shard_map/ppermute | solution.py:350
  36.5 27.8 %fused_step.1 = (bf16[512,1792]{1,0:T(8,128)(2,1)}, bf16[1792,2048]{1,0:T(8,128)(2,1)}, f32[1792,2048]{1,0:T(8,128)}) custom-call(bf16[512,2048]{1,0:T(8,128)(2,1)} %bitcast.3, bf16[512,1792]{1,0:T(8,128)(2,1)} %bitcast.5, f32[1792,2048]{1,0:T(8,128)} %w_ref.1, f32[1792,2048]{1,0:T(8,128)} %m_ref.1, f32[1792,2048]{1,0:T(8,128)} %s_ref.1), custom_call_target="tpu_custom_call" | custom-call | flops 7516192768 | bytes 66060288 | tf_op jit(solution)/shard_map/fused_step/pallas_call | solution.py:175
  64.3 0.0 collective-permute-done.refs_1_
  64.3 0.0 copy-start
  64.3 0.0 collective-permute-done.1.refs_2_
  64.4 0.0 copy-start.1
  64.4 0.0 collective-permute-done.2.refs_3_
  64.4 0.0 copy-start.2
  64.4 0.7 copy-done
  65.1 0.1 copy-done.1
  65.3 0.2 copy-done.2
  65.4 33.6 %reduce_both.1 = (bf16[128,1792]{1,0:T(8,128)(2,1)}, bf16[64,2048]{1,0:T(8,128)(2,1)}) custom-call(bf16[2,2,128,1792]{3,2,1,0:T(8,128)(2,1)} %bitcast.4, bf16[1792,2048]{1,0:T(8,128)(2,1)} %get-tuple-element.17.fresh_hbm, bf16[128,1792]{1,0:T(8,128)(2,1)} %refs_0_, bf16[128,1792]{1,0:T(8,128)(2,1)} %copy-done, bf16[128,1792]{1,0:T(8,128)(2,1)} %copy-done.1, ...), custom_call_target="tpu_custom_call" | custom-call | tf_op jit(solution)/shard_map/reduce_both/pallas_call | solution.py:317
  99.0 1.8 %copy.11 = bf16[128,1792]{1,0:T(8,128)(2,1)} copy(bf16[128,1792]{1,0:T(8,128)(2,1)} %get-tuple-element.25) | data formatting | bytes 917504
  100.8 1.7 %copy.12 = bf16[64,2048]{1,0:T(8,128)(2,1)} copy(bf16[64,2048]{1,0:T(8,128)(2,1)} %get-tuple-element.26) | data formatting | bytes 524288
Async XLA Ops:
  32.1 32.3 %collective-permute-start = (bf16[128,1792]{1,0:T(8,128)(2,1)}, bf16[128,1792]{1,0:T(8,128)(2,1)S(1)}, u32[]{:S(2)}, u32[]{:S(2)}) collective-permute-start(bf16[128,1792]{1,0:T(8,128)(2,1)} %refs_0_), channel_id=1, source_target_pairs={{0,1},{1,2},{2,3},{3,0},{4,5},{5,6},{6,7},{7,4},{8,9},{9,10},{10,1... | collective-permute-start | bytes 1376264 | tf_op jit(solution)/shard_map/ppermute | solution.py:350
  32.6 31.8 %collective-permute-start.1 = (bf16[128,1792]{1,0:T(8,128)(2,1)}, bf16[128,1792]{1,0:T(8,128)(2,1)S(1)}, u32[]{:S(2)}, u32[]{:S(2)}) collective-permute-start(bf16[128,1792]{1,0:T(8,128)(2,1)} %refs_0_), channel_id=1, source_target_pairs={{0,2},{1,3},{2,0},{3,1},{4,6},{5,7},{6,4},{7,5},{8,10},{9,11},{10,... | collective-permute-start | bytes 1376264 | tf_op jit(solution)/shard_map/ppermute | solution.py:350
  35.1 29.2 %collective-permute-start.2 = (bf16[128,1792]{1,0:T(8,128)(2,1)}, bf16[128,1792]{1,0:T(8,128)(2,1)S(1)}, u32[]{:S(2)}, u32[]{:S(2)}) collective-permute-start(bf16[128,1792]{1,0:T(8,128)(2,1)} %refs_0_), channel_id=1, source_target_pairs={{0,3},{1,0},{2,1},{3,2},{4,7},{5,4},{6,5},{7,6},{8,11},{9,8},{10,9... | collective-permute-start | bytes 1376264 | tf_op jit(solution)/shard_map/ppermute | solution.py:350
  64.3 0.8 copy-start
  64.4 0.9 copy-start.1
  64.4 1.1 %copy-start.2 = (bf16[128,1792]{1,0:T(8,128)(2,1)}, bf16[128,1792]{1,0:T(8,128)(2,1)S(1)}, u32[]{:S(2)}) copy-start(bf16[128,1792]{1,0:T(8,128)(2,1)S(1)} %collective-permute-done.2.refs_3_) | copy-start | bytes 1376260

commit v3 on v2

--- a/solution.py
+++ b/solution.py
@@ -336,7 +336,7 @@
         + [pltpu.VMEM(shape(j), bf16) for j in range(1, levels)]
         + [pltpu.VMEM(shape(j), f32) for j in range(1, levels)],
         compiler_params=pltpu.CompilerParams(
-            collective_id=2, has_side_effects=True, vmem_limit_bytes=62 << 20
+            collective_id=2, has_side_effects=True, vmem_limit_bytes=60 << 20
         ),
         name="reduce_both",
     )(up.reshape(chips, 2, rows, ff), fresh, *nh)

time: 103 us -> 103 us (level)
  no operation moved by 1% of the time
where the time goes in v3:
time: 103 us; the launch traced here: 102 us
  Pallas kernels  92.8 us (90%)
  local copies, waits for them, and re-layouts  4.54 us (4%)
  starting transfers between devices  4.46 us (4%)
    pallas_call x1, Pallas kernels, reduce(): pl.pallas_call(functools.partial(reduce_kernel, levels, n_dp, pieces), ou...  33.6 us
    pallas_call x1, Pallas kernels, gather(): pl.pallas_call(functools.partial(gather_kernel, n_dp, share), out_shape=[...  31.4 us
    pallas_call x1, Pallas kernels, step(): pl.pallas_call(functools.partial(step_kernel, chunk), grid=(width // bn,)...  27.8 us
    unnamed x8, local copies, waits for them, and re-layouts  4.54 us
    ppermute x3, starting transfers between devices, on_device(): lax.ppermute(later, 'dp', [(i, (i + o) % n_dp) for i in range(n_dp)])  4.46 us
  transfers between devices with their start and end apart: 3, of which 0 were waited for; matrix products, arithmetic and copies ran while one was open for 0% of the time, Pallas kernels for 27%

profile of v3, /device:TPU:0, one launch (start us, length us, event | category | flops | bytes accessed | tf_op | source)
XLA Modules:
  0.0 102.5 jit_solution(11810093106299522820)
XLA Ops:
  0.6 31.4 %gather_all.1 = (bf16[4,128,2048]{2,1,0:T(8,128)(2,1)}, bf16[4,128,1792]{2,1,0:T(8,128)(2,1)}) custom-call(bf16[128,8192]{1,0:T(8,128)(2,1)} %g.1, bf16[128,1792]{1,0:T(8,128)(2,1)} %hid.1), custom_call_target="tpu_custom_call" | custom-call | tf_op jit(solution)/shard_map/gather_all/pallas_call | solution.py:121
  32.1 0.5 collective-permute-start
  32.6 2.6 %collective-permute-start.1 = (bf16[128,1792]{1,0:T(8,128)(2,1)}, bf16[128,1792]{1,0:T(8,128)(2,1)S(1)}, u32[]{:S(2)}, u32[]{:S(2)}) collective-permute-start(bf16[128,1792]{1,0:T(8,128)(2,1)} %refs_0_), channel_id=1, source_target_pairs={{0,2},{1,3},{2,0},{3,1},{4,6},{5,7},{6,4},{7,5},{8,10},{9,11},{10,... | collective-permute-start | bytes 1376264 | tf_op jit(solution)/shard_map/ppermute | solution.py:350
  35.1 1.4 %collective-permute-start.2 = (bf16[128,1792]{1,0:T(8,128)(2,1)}, bf16[128,1792]{1,0:T(8,128)(2,1)S(1)}, u32[]{:S(2)}, u32[]{:S(2)}) collective-permute-start(bf16[128,1792]{1,0:T(8,128)(2,1)} %refs_0_), channel_id=1, source_target_pairs={{0,3},{1,0},{2,1},{3,2},{4,7},{5,4},{6,5},{7,6},{8,11},{9,8},{10,9... | collective-permute-start | bytes 1376264 | tf_op jit(solution)/shard_map/ppermute | solution.py:350
  36.5 27.8 %fused_step.1 = (bf16[512,1792]{1,0:T(8,128)(2,1)}, bf16[1792,2048]{1,0:T(8,128)(2,1)}, f32[1792,2048]{1,0:T(8,128)}) custom-call(bf16[512,2048]{1,0:T(8,128)(2,1)} %bitcast.3, bf16[512,1792]{1,0:T(8,128)(2,1)} %bitcast.5, f32[1792,2048]{1,0:T(8,128)} %w_ref.1, f32[1792,2048]{1,0:T(8,128)} %m_ref.1, f32[1792,2048]{1,0:T(8,128)} %s_ref.1), custom_call_target="tpu_custom_call" | custom-call | flops 7516192768 | bytes 66060288 | tf_op jit(solution)/shard_map/fused_step/pallas_call | solution.py:175
  64.3 0.0 collective-permute-done.refs_1_
  64.3 0.0 copy-start
  64.3 0.0 collective-permute-done.1.refs_2_
  64.4 0.0 copy-start.1
  64.4 0.0 collective-permute-done.2.refs_3_
  64.4 0.0 copy-start.2
  64.4 0.7 copy-done
  65.1 0.1 copy-done.1
  65.3 0.2 copy-done.2
  65.4 33.6 %reduce_both.1 = (bf16[128,1792]{1,0:T(8,128)(2,1)}, bf16[64,2048]{1,0:T(8,128)(2,1)}) custom-call(bf16[2,2,128,1792]{3,2,1,0:T(8,128)(2,1)} %bitcast.4, bf16[1792,2048]{1,0:T(8,128)(2,1)} %get-tuple-element.17.fresh_hbm, bf16[128,1792]{1,0:T(8,128)(2,1)} %refs_0_, bf16[128,1792]{1,0:T(8,128)(2,1)} %copy-done, bf16[128,1792]{1,0:T(8,128)(2,1)} %copy-done.1, ...), custom_call_target="tpu_custom_call" | custom-call | tf_op jit(solution)/shard_map/reduce_both/pallas_call | solution.py:317
  99.0 1.8 %copy.11 = bf16[128,1792]{1,0:T(8,128)(2,1)} copy(bf16[128,1792]{1,0:T(8,128)(2,1)} %get-tuple-element.25) | data formatting | bytes 917504
  100.8 1.7 %copy.12 = bf16[64,2048]{1,0:T(8,128)(2,1)} copy(bf16[64,2048]{1,0:T(8,128)(2,1)} %get-tuple-element.26) | data formatting | bytes 524288
Async XLA Ops:
  32.1 32.3 %collective-permute-start = (bf16[128,1792]{1,0:T(8,128)(2,1)}, bf16[128,1792]{1,0:T(8,128)(2,1)S(1)}, u32[]{:S(2)}, u32[]{:S(2)}) collective-permute-start(bf16[128,1792]{1,0:T(8,128)(2,1)} %refs_0_), channel_id=1, source_target_pairs={{0,1},{1,2},{2,3},{3,0},{4,5},{5,6},{6,7},{7,4},{8,9},{9,10},{10,1... | collective-permute-start | bytes 1376264 | tf_op jit(solution)/shard_map/ppermute | solution.py:350
  32.6 31.8 %collective-permute-start.1 = (bf16[128,1792]{1,0:T(8,128)(2,1)}, bf16[128,1792]{1,0:T(8,128)(2,1)S(1)}, u32[]{:S(2)}, u32[]{:S(2)}) collective-permute-start(bf16[128,1792]{1,0:T(8,128)(2,1)} %refs_0_), channel_id=1, source_target_pairs={{0,2},{1,3},{2,0},{3,1},{4,6},{5,7},{6,4},{7,5},{8,10},{9,11},{10,... | collective-permute-start | bytes 1376264 | tf_op jit(solution)/shard_map/ppermute | solution.py:350
  35.1 29.2 %collective-permute-start.2 = (bf16[128,1792]{1,0:T(8,128)(2,1)}, bf16[128,1792]{1,0:T(8,128)(2,1)S(1)}, u32[]{:S(2)}, u32[]{:S(2)}) collective-permute-start(bf16[128,1792]{1,0:T(8,128)(2,1)} %refs_0_), channel_id=1, source_target_pairs={{0,3},{1,0},{2,1},{3,2},{4,7},{5,4},{6,5},{7,6},{8,11},{9,8},{10,9... | collective-permute-start | bytes 1376264 | tf_op jit(solution)/shard_map/ppermute | solution.py:350
  64.3 0.8 copy-start
  64.4 0.9 copy-start.1
  64.4 1.1 %copy-start.2 = (bf16[128,1792]{1,0:T(8,128)(2,1)}, bf16[128,1792]{1,0:T(8,128)(2,1)S(1)}, u32[]{:S(2)}) copy-start(bf16[128,1792]{1,0:T(8,128)(2,1)S(1)} %collective-permute-done.2.refs_3_) | copy-start | bytes 1376260
